TPU v7x, 128 devices: a whole 4x4x4 slice. The times are simulated.
128 devices in a mesh: frame: 16 (over y, x), head: 8 (over z, core).
Axes of the slice: x: 4, y: 4, z: 4, core: 2. Of those that a mesh axis runs over, the one named last changes fastest.
Arguments:
- tokens: bfloat16 [12288, 5120], P('frame', 'head'), may hold values from -40 to 40
- mask_block_frame: int32 [96], replicated, may hold values from 0 to 7, as said below
- attended_key_blocks: int32 [96, 10], replicated, may hold values from 0 to 95, as said below
- frozen_query_key_value: bfloat16 [5120, 3, 3072], P(None, None, 'head'), may hold values from -0.104815686 to 0.104815686
- query_key_value_down_weight: bfloat16 [5120, 192], replicated, may hold values from -0.078125 to 0.078125
- query_key_value_up_weight: bfloat16 [64, 3, 3072], P(None, None, 'head'), may hold values from -0.375 to 0.375
- frozen_output_weight: bfloat16 [3072, 5120], P('head'), may hold values from -0.109375 to 0.109375
- output_down_weight: bfloat16 [3072, 64], P('head'), may hold values from -0.109375 to 0.109375
- output_up_weight: bfloat16 [64, 5120], P(None, 'head'), may hold values from -0.75 to 0.75
Outputs:
- attended_out: bfloat16 [12288, 5120], P('frame', 'head')
Inputs may be any that keep to these rules, and one draw needn't show every extreme that they name: `mask_block_frame`: Non-decreasing along the blocks; every frame from 0 to 7 holds at least one block. `attended_key_blocks`: row b lists 10 distinct key blocks and always includes b itself. Take aligned groups of 6 blocks; for a group of query blocks and another group g groups away (g >= 1), the rows of the first group together name exactly 4 // 2 ** (g - 1) distinct blocks of the second, except that a group exactly 8 groups away is named by exactly the larger of that number and 2.
All inputs are finite; a program needn't handle non-finite values.
Results may differ from a plain program's by a relative error of at most 0.017.
Values may be sent and summed in bfloat16 or wider, within the bound.
A program may use at most 128 MiB of HBM per device.

v0:
```python
import math
import jax
import jax.numpy as jnp
from jax import lax
from jax.sharding import PartitionSpec as P

MODEL_WIDTH = 5120
HEAD_SIZE = 128
BLOCK = 128


def rotate_pairs(values, frame_pos, place):
    time_pairs = (HEAD_SIZE - 4 * (HEAD_SIZE // 6)) // 2
    space_pairs = (HEAD_SIZE - 2 * time_pairs) // 2
    time_freq = 10000.0 ** (-jnp.arange(time_pairs).astype(jnp.float32) / time_pairs)
    space_freq = 10000.0 ** (-jnp.arange(space_pairs).astype(jnp.float32) / space_pairs)
    time_angle = frame_pos[:, None] * time_freq[None, :]
    space_angle = place[:, None] * space_freq[None, :]
    cos_time = jnp.cos(time_angle)[:, None, :]
    sin_time = jnp.sin(time_angle)[:, None, :]
    cos_space = jnp.cos(space_angle)[:, None, :]
    sin_space = jnp.sin(space_angle)[:, None, :]
    first_part = values[:, :, :time_pairs]
    second_part = values[:, :, time_pairs : 2 * time_pairs]
    third_part = values[:, :, 2 * time_pairs : 2 * time_pairs + space_pairs]
    fourth_part = values[:, :, 2 * time_pairs + space_pairs :]
    return jnp.concatenate(
        [
            first_part * cos_time - second_part * sin_time,
            first_part * sin_time + second_part * cos_time,
            third_part * cos_space - fourth_part * sin_space,
            third_part * sin_space + fourth_part * cos_space,
        ],
        axis=-1,
    )


def token_positions(mask_block_frame, block_ids):
    count_blocks = mask_block_frame.shape[0]
    all_blocks = jnp.arange(count_blocks)
    same_frame = mask_block_frame[:, None] == mask_block_frame[None, :]
    first_block = jnp.min(jnp.where(same_frame, all_blocks[None, :], count_blocks), axis=1)
    inner_ids = jnp.arange(BLOCK)
    token_ids = block_ids[:, None] * BLOCK + inner_ids[None, :]
    frame_pos = (
        jnp.broadcast_to(mask_block_frame[block_ids][:, None], token_ids.shape)
        .reshape(-1)
        .astype(jnp.float32)
    )
    place = (token_ids - first_block[block_ids][:, None] * BLOCK).reshape(-1).astype(jnp.float32)
    return (frame_pos, place)


def body(
    tokens,
    mask_block_frame,
    attended_key_blocks,
    frozen_query_key_value,
    query_key_value_down_weight,
    query_key_value_up_weight,
    frozen_output_weight,
    output_down_weight,
    output_up_weight,
):
    tok_rows = tokens.shape[0]
    blocks_here = tok_rows // BLOCK
    local_width = frozen_output_weight.shape[0]
    heads_here = local_width // HEAD_SIZE
    adapter_rank_width = output_up_weight.shape[0]
    listed = attended_key_blocks.shape[1]
    weights_flat = frozen_query_key_value.reshape(MODEL_WIDTH, 3 * local_width)
    rank_segment = lax.all_gather(tokens, "head", axis=1, tiled=True)
    projected_rows = jnp.dot(rank_segment, weights_flat, preferred_element_type=jnp.float32)
    adapter_output_sum = jnp.dot(
        rank_segment, query_key_value_down_weight, preferred_element_type=jnp.float32
    )
    adapter_query_key_value = adapter_output_sum.astype(jnp.bfloat16).reshape(
        tok_rows, 3, adapter_rank_width
    )
    projected_rows = projected_rows.reshape(tok_rows, 3, local_width) + jnp.einsum(
        "ngc,cgz->ngz",
        adapter_query_key_value,
        query_key_value_up_weight,
        preferred_element_type=jnp.float32,
    )
    frame_index = lax.axis_index("frame")
    block_ids = frame_index * blocks_here + jnp.arange(blocks_here, dtype=jnp.int32)
    frame_pos, place = token_positions(mask_block_frame, block_ids)
    queries = rotate_pairs(
        projected_rows[:, 0].reshape(tok_rows, heads_here, HEAD_SIZE), frame_pos, place
    ).astype(jnp.bfloat16)
    keys = rotate_pairs(
        projected_rows[:, 1].reshape(tok_rows, heads_here, HEAD_SIZE), frame_pos, place
    ).astype(jnp.bfloat16)
    key_tiles = keys.reshape(blocks_here, BLOCK, local_width)
    value_tiles = projected_rows[:, 2].astype(jnp.bfloat16).reshape(blocks_here, BLOCK, local_width)
    my_lists = lax.dynamic_slice_in_dim(
        attended_key_blocks, frame_index * blocks_here, blocks_here, 0
    )
    pool_keys, pool_values = (
        lax.all_gather(key_tiles, "frame", axis=0, tiled=True),
        lax.all_gather(value_tiles, "frame", axis=0, tiled=True),
    )
    chosen_keys = pool_keys[my_lists].reshape(blocks_here, listed * BLOCK, heads_here, HEAD_SIZE)
    chosen_values = pool_values[my_lists].reshape(
        blocks_here, listed * BLOCK, heads_here, HEAD_SIZE
    )
    query_tiles = queries.reshape(blocks_here, BLOCK, heads_here, HEAD_SIZE)
    scores = jnp.einsum(
        "nqhd,nkhd->nhqk", query_tiles, chosen_keys, preferred_element_type=jnp.float32
    ) / math.sqrt(HEAD_SIZE)
    row_max = jnp.max(scores, axis=-1, keepdims=True)
    powers = jnp.exp(scores - row_max)
    probs = (powers / jnp.sum(powers, axis=-1, keepdims=True)).astype(jnp.bfloat16)
    attention_result = jnp.einsum(
        "nhqk,nkhd->nqhd", probs, chosen_values, preferred_element_type=jnp.float32
    ).astype(jnp.bfloat16)
    attention_result = attention_result.reshape(tok_rows, local_width)
    adapter_output = lax.psum(
        jnp.dot(attention_result, output_down_weight, preferred_element_type=jnp.float32).astype(
            jnp.bfloat16
        ),
        "head",
    )
    partial_value = jnp.dot(
        attention_result, frozen_output_weight, preferred_element_type=jnp.float32
    )
    frozen_output = lax.psum_scatter(
        partial_value.astype(jnp.bfloat16), "head", scatter_dimension=1, tiled=True
    ).astype(jnp.float32)
    return (
        frozen_output
        + jnp.dot(adapter_output, output_up_weight, preferred_element_type=jnp.float32)
    ).astype(jnp.bfloat16)


def solution(mesh):
    return jax.shard_map(
        body,
        mesh=mesh,
        in_specs=(
            P("frame", "head"),
            P(),
            P(),
            P(None, None, "head"),
            P(),
            P(None, None, "head"),
            P("head", None),
            P("head", None),
            P(None, "head"),
        ),
        out_specs=P("frame", "head"),
        check_vma=False,
    )
```

profile of v0, /device:TPU:0, one launch (start us, length us, event | category | flops | bytes accessed | tf_op | source)
XLA Modules:
  0.0 407.3 jit_solution(18228735309528296065)
XLA Ops:
  6.5 0.0 copy-start
  6.5 0.0 all-gather.4.cloned.1.call-start
  6.5 0.7 all-gather.4.cloned.1.call-update
  7.3 0.0 all-gather.8.cloned.1.call-start
  7.3 1.3 gather_fusion.1
  8.6 0.9 select_reduce_fusion
  9.6 0.6 gather_fusion.2
  10.2 16.2 %copy.37 = bf16[5120,3,384]{0,2,1:T(8,128)(2,1)} copy(bf16[5120,3,384]{2,0,1:T(8,128)(2,1)} %param.12) | data formatting | bytes 23592960 | tf_op args[3]
  26.4 0.1 broadcast_bitcast_fusion
  26.5 0.1 convert_bitcast_fusion
  26.6 0.3 multiply_cosine_fusion.1
  26.9 0.6 multiply_cosine_fusion
  27.5 0.0 copy-start.4
  27.5 31.6 %all-gather.4.cloned.1.call-done = bf16[768,5120]{1,0:T(8,128)(2,1)} async-done(((bf16[768,640]{1,0:T(8,128)(2,1)}), bf16[768,5120]{1,0:T(8,128)(2,1)}) %all-gather.4.cloned.1.call-update) | async-done | bytes 7864336 | tf_op jit(solution)/shard_map/all_gather | solution.py:72
  59.2 6.1 %convolution_convert_fusion.1 = bf16[768,192]{0,1:T(8,128)(2,1)S(1)} fusion(bf16[768,5120]{1,0:T(8,128)(2,1)} %all-gather.4.cloned.1.call-done, bf16[5120,192]{0,1:T(8,128)(2,1)S(1)} %copy-done), kind=kOutput, calls=%fused_computation.22 | convolution fusion | flops 1510096896 | bytes 10125312 | tf_op jit(solution)/shard_map/dot_general | solution.py:74
  65.3 0.7 fusion.38
  66.0 13.3 %bitcast_add_fusion = f32[768,3,384]{0,2,1:T(8,128)S(1)} fusion(f32[3,768,384]{1,2,0:T(8,128)S(1)} %fusion.38, bf16[5120,3,384]{0,2,1:T(8,128)(2,1)S(1)} %copy-done.2, bf16[768,5120]{1,0:T(8,128)(2,1)} %all-gather.4.cloned.1.call-done), kind=kOutput, calls=%fused_computation.18 | convolution fusion | flops 9060581376 | bytes 26738688 | tf_op jit(solution)/shard_map/dot_general | solution.py:73
  79.3 0.2 fusion.36
  79.5 0.0 copy-start.7
  79.5 0.3 subtract_convert_fusion.1
  79.8 0.1 subtract_convert_fusion.3
  80.0 1.1 copy-done.3
  81.0 0.2 pad_maximum_fusion
  81.2 0.7 convert_element_type.81
  81.9 1.3 copy.45
  83.1 0.0 all-gather.8.cloned.1.call-update
  83.1 0.0 all-gather.6.cloned.1.call-start
  83.2 1.3 slice.81
  84.5 1.1 copy.38
  85.6 0.0 all-gather.6.cloned.1.call-update
  85.6 0.2 reduce-scatter.4.cloned.1.call-start
  85.9 0.1 compare_select_fusion
  85.9 0.1 copy.39
  86.0 0.1 reshape.205
  86.1 0.2 concatenate.19
  86.4 0.4 copy.43
  86.8 0.2 concatenate.20
  87.0 0.4 copy.44
  87.5 0.1 concatenate.17
  87.6 0.4 copy.41
  88.0 0.1 concatenate.18
  88.1 0.4 copy.42
  88.5 70.3 %all-gather.8.cloned.1.call-done = bf16[96,128,384]{2,1,0:T(8,128)(2,1)} async-done(((bf16[6,128,384]{2,1,0:T(8,128)(2,1)}), bf16[96,128,384]{2,1,0:T(8,128)(2,1)}) %all-gather.8.cloned.1.call-update) | async-done | bytes 9437200 | tf_op jit(solution)/shard_map/all_gather | solution.py:101
  158.8 7.7 %gather_fusion.3 = bf16[60,128,384]{2,1,0:T(8,128)(2,1)} fusion(bf16[96,128,384]{2,1,0:T(8,128)(2,1)} %all-gather.8.cloned.1.call-done, s32[1024]{0:T(1024)S(1)} %pad_clamp_fusion.1), kind=kCustom, calls=%fused_computation.3 | custom fusion | bytes 11796720 | tf_op jit(solution)/shard_map/gather | solution.py:104
  166.5 15.9 %reshape.243 = bf16[6,1280,3,128]{3,2,1,0:T(4,128)(2,1)} reshape(bf16[60,128,384]{2,1,0:T(8,128)(2,1)} %gather_fusion.3) | data formatting | bytes 11796480 | tf_op jit(solution)/shard_map/reshape | solution.py:104
  182.4 9.4 %fusion.7 = f32[6,3,128,1280]{3,2,1,0:T(8,128)} fusion(bf16[6,1280,3,128]{3,2,1,0:T(4,128)(2,1)} %reshape.243, bf16[6,128,3,42]{3,1,2,0:T(8,128)(2,1)S(1)} %copy.44, bf16[6,128,3,42]{3,1,2,0:T(8,128)(2,1)S(1)} %copy.43, bf16[6,128,3,22]{3,1,2,0:T(8,128)(2,1)S(1)} %copy.42, bf16[6,128,3,22]{3,1,2,0:T(8,128)(2,1)S(1)} %copy.41), kind=kOutput, calls=%fused_computation.13 | convolution fusion | flops 757334016 | bytes 18284544 | tf_op jit(solution)/shard_map/nqhd,nkhd->nhqk/dot_general | solution.py:109
  191.8 15.6 %fusion.37 = (f32[6,3,128]{2,1,0:T(4,128)S(1)}, f32[6,3,128,1280]{3,2,1,0:T(8,128)}) fusion(f32[6,3,128,1280]{3,2,1,0:T(8,128)} %fusion.7), kind=kOutput, calls=%fused_computation.64 | output fusion | flops 11797759 | bytes 23602176 | tf_op jit(solution)/shard_map/sub | solution.py:113
  207.4 28.7 %all-gather.6.cloned.1.call-done = bf16[96,128,384]{2,1,0:T(8,128)(2,1)} async-done(((bf16[6,128,384]{2,1,0:T(8,128)(2,1)}), bf16[96,128,384]{2,1,0:T(8,128)(2,1)}) %all-gather.6.cloned.1.call-update) | async-done | bytes 9437200 | tf_op jit(solution)/shard_map/all_gather | solution.py:102
  236.1 7.8 %gather_fusion = bf16[60,128,384]{2,1,0:T(8,128)(2,1)} fusion(bf16[96,128,384]{2,1,0:T(8,128)(2,1)} %all-gather.6.cloned.1.call-done, s32[1024]{0:T(1024)S(1)} %pad_clamp_fusion.1), kind=kCustom, calls=%fused_computation | custom fusion | bytes 11796720 | tf_op jit(solution)/shard_map/gather | solution.py:105
  243.9 15.8 %reshape.242 = bf16[6,1280,3,128]{3,2,1,0:T(4,128)(2,1)} reshape(bf16[60,128,384]{2,1,0:T(8,128)(2,1)} %gather_fusion) | data formatting | bytes 11796480 | tf_op jit(solution)/shard_map/reshape | solution.py:105
  259.7 9.2 %fusion.19 = bf16[6,128,3,128]{1,3,2,0:T(8,128)(2,1)S(1)} fusion(f32[6,3,128,1280]{3,2,1,0:T(8,128)} %get-tuple-element.24, f32[6,3,128]{2,1,0:T(4,128)S(1)} %get-tuple-element.23, bf16[6,1280,3,128]{3,2,1,0:T(4,128)(2,1)} %reshape.242), kind=kOutput, calls=%fused_computation.21 | convolution fusion | flops 761167872 | bytes 18293760 | tf_op jit(solution)/shard_map/nhqk,nkhd->nqhd/dot_general | solution.py:115
  268.9 0.4 copy.49
  269.3 8.8 %convolution_convert_fusion = bf16[768,5120]{1,0:T(8,128)(2,1)} fusion(bf16[384,5120]{1,0:T(8,128)(2,1)} %param.15, bf16[48,8,6,128]{3,2,1,0:T(8,128)(2,1)S(1)} %bitcast.62), kind=kOutput, calls=%fused_computation.11 | convolution fusion | flops 3023831040 | bytes 12386304 | tf_op jit(solution)/shard_map/dot_general | solution.py:125
  278.1 10.6 %copy.54 = bf16[768,5120]{0,1:T(8,128)(2,1)} copy(bf16[768,5120]{1,0:T(8,128)(2,1)} %convolution_convert_fusion) | data formatting | bytes 15728640
  288.8 0.0 reduce-scatter.4.cloned.1.call-update
  288.8 0.0 all-reduce.2.cloned.1.call-start
  288.9 0.7 copy-done.6
  289.6 0.9 convolution_convert_fusion.2
  290.4 0.0 all-reduce.2.cloned.1.call-update
  290.5 48.4 %reduce-scatter.4.cloned.1.call-done = bf16[640,768]{1,0:T(8,128)(2,1)} async-done(((bf16[5120,768]{1,0:T(8,128)(2,1)}), bf16[640,768]{1,0:T(8,128)(2,1)}) %reduce-scatter.4.cloned.1.call-update) | async-done | bytes 983056
  338.9 1.5 copy.55
  340.4 58.1 %all-reduce.2.cloned.1.call-done = bf16[768,64]{0,1:T(8,128)(2,1)} async-done(((bf16[768,64]{0,1:T(8,128)(2,1)}), bf16[768,64]{0,1:T(8,128)(2,1)}) %all-reduce.2.cloned.1.call-update) | async-done | bytes 98320 | tf_op jit(solution)/shard_map/psum | solution.py:119
  398.5 0.0 copy-done.5
  398.5 2.3 add_convert_fusion
  (17 shorter events, 0.1 us)
Async XLA Ops:
  6.5 52.6 %copy-start = (bf16[5120,192]{0,1:T(8,128)(2,1)S(1)}, bf16[5120,192]{0,1:T(8,128)(2,1)}, u32[]{:S(2)}) copy-start(bf16[5120,192]{0,1:T(8,128)(2,1)} %param.13) | copy-start | bytes 5898244
  6.5 52.6 %all-gather.4.cloned.1.call-start = ((), (), s32[]{:S(2)}) async-start(), calls=%async_computation.1 | async-start | bytes 8847360 | tf_op jit(solution)/shard_map/all_gather | solution.py:72
  7.3 151.5 %all-gather.8.cloned.1.call-start = ((), (), s32[]{:S(2)}) async-start(), calls=%async_computation.3 | async-start | bytes 10027008 | tf_op jit(solution)/shard_map/all_gather | solution.py:101
  27.5 37.8 %copy-start.4 = (bf16[64,3,384]{2,0,1:T(8,128)(2,1)S(1)}, bf16[64,3,384]{2,0,1:T(8,128)(2,1)}, u32[]{:S(2)}) copy-start(bf16[64,3,384]{2,0,1:T(8,128)(2,1)} %param.14) | copy-start | bytes 442372
  59.2 6.8 %copy-start.2 = (bf16[5120,3,384]{0,2,1:T(8,128)(2,1)S(1)}, bf16[5120,3,384]{0,2,1:T(8,128)(2,1)}, u32[]{:S(2)}) copy-start(bf16[5120,3,384]{0,2,1:T(8,128)(2,1)} %copy.37) | copy-start | bytes 35389444
  79.3 1.7 copy-start.3
  79.5 6.4 %copy-start.7 = (s32[96,10]{0,1:T(8,128)S(1)}, s32[96,10]{0,1:T(8,128)}, u32[]{:S(2)}) copy-start(s32[96,10]{0,1:T(8,128)} %param.11) | copy-start | bytes 11524
  83.1 152.9 %all-gather.6.cloned.1.call-start = ((), (), s32[]{:S(2)}) async-start(), calls=%async_computation.2 | async-start | bytes 10027008 | tf_op jit(solution)/shard_map/all_gather | solution.py:102
  85.6 253.2 %reduce-scatter.4.cloned.1.call-start = ((), (), s32[]{:S(2)}) async-start(), calls=%async_computation.5 | async-start | bytes 8847360
  288.8 0.8 copy-start.6
  288.8 109.7 %copy-start.5 = (bf16[64,640]{1,0:T(8,128)(2,1)S(1)}, bf16[64,640]{1,0:T(8,128)(2,1)}, u32[]{:S(2)}) copy-start(bf16[64,640]{1,0:T(8,128)(2,1)} %param.17) | copy-start | bytes 245764
  288.8 112.0 %copy-start.1 = (bf16[5120,192]{0,1:T(8,128)(2,1)S(1)}, bf16[5120,192]{0,1:T(8,128)(2,1)}, u32[]{:S(2)}) copy-start(bf16[5120,192]{0,1:T(8,128)(2,1)} %param.13) | copy-start | bytes 5898244
  288.8 109.7 %all-reduce.2.cloned.1.call-start = ((), (), s32[]{:S(2)}) async-start(), calls=%async_computation.4 | async-start | bytes 196608 | tf_op jit(solution)/shard_map/psum | solution.py:119
Sparse Core Ops, SparseCore 0:
  9.0 50.0 all-gather.3
  83.3 75.4 all-gather.7
  160.9 75.1 all-gather.5
  288.9 49.8 reduce-scatter.3
  341.0 57.4 all-reduce.1
where the time goes:
time: 409 us; the launch traced here: 407 us
  waiting for transfers between devices  238 us (58%)
  local copies, waits for them, and re-layouts  86.9 us (21%)
  matrix products  50.6 us (12%)
  other arithmetic  18.3 us (4%)
  between operations  13.3 us (3%)
    all_gather x1, waiting for transfers between devices, body(): lax.all_gather(key_tiles, 'frame', axis=0, tiled=True)  70.3 us
    psum x1, waiting for transfers between devices, body(): lax.psum(jnp.dot(attention_result, output_down_weight, preferred_element_...  58.1 us
    unnamed x6, waiting for transfers between devices  49.2 us
    all_gather x1, waiting for transfers between devices, body(): rank_segment = lax.all_gather(tokens, 'head', axis=1, tiled=True)  31.6 us
    unnamed x19, local copies, waits for them, and re-layouts  30.2 us
    all_gather x1, waiting for transfers between devices, body(): lax.all_gather(value_tiles, 'frame', axis=0, tiled=True)  28.7 us
    reshape x1, local copies, waits for them, and re-layouts, body(): pool_keys[my_lists]  15.9 us
    reshape x1, local copies, waits for them, and re-layouts, body(): pool_values[my_lists]  15.8 us
  transfers between devices with their start and end apart: 5, of which 5 were waited for; matrix products, arithmetic and copies ran while one was open for 19% of the time, Pallas kernels for 0%

commit v1 on v0

--- a/solution.py
+++ b/solution.py
@@ -7,6 +7,12 @@
 MODEL_WIDTH = 5120
 HEAD_SIZE = 128
 BLOCK = 128
+
+
+def summed_here(x, mesh_axis):
+    pieces = lax.all_gather(x, mesh_axis, axis=0, tiled=False)
+    acc = pieces.sum(axis=0)
+    return acc
 
 
 def rotate_pairs(values, frame_pos, place):
@@ -116,7 +122,7 @@
         "nhqk,nkhd->nqhd", probs, chosen_values, preferred_element_type=jnp.float32
     ).astype(jnp.bfloat16)
     attention_result = attention_result.reshape(tok_rows, local_width)
-    adapter_output = lax.psum(
+    adapter_output = summed_here(
         jnp.dot(attention_result, output_down_weight, preferred_element_type=jnp.float32).astype(
             jnp.bfloat16
         ),

time: 409 us -> 351 us (0.86)
  waiting for transfers between devices: 238 us -> 166 us
  blocking collectives: 0 us -> 14.6 us
    psum x1 -> x0, waiting for transfers between devices: 58.1 us -> none  [body(): lax.psum(jnp.dot(attention_result, output_down_weight, preferred_element_...]
    all_gather x0 -> x1, blocking collectives: none -> 14.6 us  [summed_here(): pieces = lax.all_gather(x, mesh_axis, axis=0, tiled=False)]
    unnamed x6 -> x5, waiting for transfers between devices: 49.2 us -> 35.5 us
    unnamed x19 -> x20, local copies, waits for them, and re-layouts: 30.2 us -> 30.3 us
  transfers between devices with their start and end apart: 5 -> 4, of which waited for: 5 -> 4; matrix products, arithmetic and copies ran while one was open for 19% -> 21% of each run, Pallas kernels for 0% -> 0%
where the time goes in v1:
time: 351 us; the launch traced here: 349 us
  waiting for transfers between devices  166 us (47%)
  local copies, waits for them, and re-layouts  87 us (25%)
  matrix products  49.1 us (14%)
  other arithmetic  18.9 us (5%)
  blocking collectives  14.6 us (4%)
  between operations  13.4 us (4%)
    all_gather x1, waiting for transfers between devices, body(): lax.all_gather(key_tiles, 'frame', axis=0, tiled=True)  70.2 us
    unnamed x5, waiting for transfers between devices  35.5 us
    all_gather x1, waiting for transfers between devices, body(): rank_segment = lax.all_gather(tokens, 'head', axis=1, tiled=True)  31.7 us
    unnamed x20, local copies, waits for them, and re-layouts  30.3 us
    all_gather x1, waiting for transfers between devices, body(): lax.all_gather(value_tiles, 'frame', axis=0, tiled=True)  28.7 us
    reshape x1, local copies, waits for them, and re-layouts, body(): pool_keys[my_lists]  15.9 us
    reshape x1, local copies, waits for them, and re-layouts, body(): pool_values[my_lists]  15.8 us
    sub x1, other arithmetic, body(): powers = jnp.exp(scores - row_max)  15.6 us
  transfers between devices with their start and end apart: 4, of which 4 were waited for; matrix products, arithmetic and copies ran while one was open for 21% of the time, Pallas kernels for 0%

profile of v1, /device:TPU:0, one launch (start us, length us, event | category | flops | bytes accessed | tf_op | source)
XLA Modules:
  0.0 349.4 jit_solution(8704891268743575743)
XLA Ops:
  6.5 0.0 copy-start
  6.5 0.0 all-gather.5.cloned.1.call-start
  6.5 0.7 all-gather.5.cloned.1.call-update
  7.3 0.0 all-gather.9.cloned.1.call-start
  7.3 1.3 gather_fusion.1
  8.6 0.9 select_reduce_fusion
  9.6 0.6 gather_fusion.2
  10.2 16.1 %copy.37 = bf16[5120,3,384]{0,2,1:T(8,128)(2,1)} copy(bf16[5120,3,384]{2,0,1:T(8,128)(2,1)} %param.12) | data formatting | bytes 23592960 | tf_op args[3]
  26.3 0.1 broadcast_bitcast_fusion
  26.4 0.1 convert_bitcast_fusion
  26.5 0.3 multiply_cosine_fusion.1
  26.8 0.6 multiply_cosine_fusion
  27.4 0.0 copy-start.4
  27.4 31.7 %all-gather.5.cloned.1.call-done = bf16[768,5120]{1,0:T(8,128)(2,1)} async-done(((bf16[768,640]{1,0:T(8,128)(2,1)}), bf16[768,5120]{1,0:T(8,128)(2,1)}) %all-gather.5.cloned.1.call-update) | async-done | bytes 7864336 | tf_op jit(solution)/shard_map/all_gather | solution.py:78
  59.2 0.0 copy-done
  59.2 6.1 %convolution_convert_fusion.1 = bf16[768,192]{0,1:T(8,128)(2,1)S(1)} fusion(bf16[768,5120]{1,0:T(8,128)(2,1)} %all-gather.5.cloned.1.call-done, bf16[5120,192]{0,1:T(8,128)(2,1)S(1)} %copy-done), kind=kOutput, calls=%fused_computation.22 | convolution fusion | flops 1510096896 | bytes 10125312 | tf_op jit(solution)/shard_map/dot_general | solution.py:80
  65.3 0.7 fusion.38
  66.0 13.3 %bitcast_add_fusion = f32[768,3,384]{0,2,1:T(8,128)S(1)} fusion(f32[3,768,384]{1,2,0:T(8,128)S(1)} %fusion.38, bf16[5120,3,384]{0,2,1:T(8,128)(2,1)S(1)} %copy-done.2, bf16[768,5120]{1,0:T(8,128)(2,1)} %all-gather.5.cloned.1.call-done), kind=kOutput, calls=%fused_computation.18 | convolution fusion | flops 9060581376 | bytes 26738688 | tf_op jit(solution)/shard_map/dot_general | solution.py:79
  79.3 0.2 fusion.36
  79.5 0.0 copy-start.7
  79.5 0.3 subtract_convert_fusion.1
  79.8 0.1 subtract_convert_fusion.3
  80.0 1.1 copy-done.3
  81.0 0.2 pad_maximum_fusion
  81.2 0.7 convert_element_type.83
  81.9 1.3 copy.45
  83.1 0.0 all-gather.9.cloned.1.call-update
  83.2 0.0 all-gather.7.cloned.1.call-start
  83.2 1.3 slice.81
  84.5 1.1 copy.38
  85.6 0.0 all-gather.7.cloned.1.call-update
  85.6 0.2 reduce-scatter.4.cloned.1.call-start
  85.9 0.1 compare_select_fusion
  85.9 0.1 copy.39
  86.0 0.1 reshape.205
  86.1 0.2 concatenate.19
  86.4 0.4 copy.43
  86.8 0.2 concatenate.20
  87.1 0.4 copy.44
  87.5 0.1 concatenate.17
  87.6 0.4 copy.41
  88.0 0.1 concatenate.18
  88.1 0.4 copy.42
  88.5 70.2 %all-gather.9.cloned.1.call-done = bf16[96,128,384]{2,1,0:T(8,128)(2,1)} async-done(((bf16[6,128,384]{2,1,0:T(8,128)(2,1)}), bf16[96,128,384]{2,1,0:T(8,128)(2,1)}) %all-gather.9.cloned.1.call-update) | async-done | bytes 9437200 | tf_op jit(solution)/shard_map/all_gather | solution.py:107
  158.8 7.7 %gather_fusion.3 = bf16[60,128,384]{2,1,0:T(8,128)(2,1)} fusion(bf16[96,128,384]{2,1,0:T(8,128)(2,1)} %all-gather.9.cloned.1.call-done, s32[1024]{0:T(1024)S(1)} %pad_clamp_fusion.1), kind=kCustom, calls=%fused_computation.3 | custom fusion | bytes 11796720 | tf_op jit(solution)/shard_map/gather | solution.py:110
  166.5 15.9 %reshape.244 = bf16[6,1280,3,128]{3,2,1,0:T(4,128)(2,1)} reshape(bf16[60,128,384]{2,1,0:T(8,128)(2,1)} %gather_fusion.3) | data formatting | bytes 11796480 | tf_op jit(solution)/shard_map/reshape | solution.py:110
  182.4 9.4 %fusion.7 = f32[6,3,128,1280]{3,2,1,0:T(8,128)} fusion(bf16[6,1280,3,128]{3,2,1,0:T(4,128)(2,1)} %reshape.244, bf16[6,128,3,42]{3,1,2,0:T(8,128)(2,1)S(1)} %copy.44, bf16[6,128,3,42]{3,1,2,0:T(8,128)(2,1)S(1)} %copy.43, bf16[6,128,3,22]{3,1,2,0:T(8,128)(2,1)S(1)} %copy.42, bf16[6,128,3,22]{3,1,2,0:T(8,128)(2,1)S(1)} %copy.41), kind=kOutput, calls=%fused_computation.13 | convolution fusion | flops 757334016 | bytes 18284544 | tf_op jit(solution)/shard_map/nqhd,nkhd->nhqk/dot_general | solution.py:115
  191.7 15.6 %fusion.37 = (f32[6,3,128]{2,1,0:T(4,128)S(1)}, f32[6,3,128,1280]{3,2,1,0:T(8,128)}) fusion(f32[6,3,128,1280]{3,2,1,0:T(8,128)} %fusion.7), kind=kOutput, calls=%fused_computation.65 | output fusion | flops 11797759 | bytes 23602176 | tf_op jit(solution)/shard_map/sub | solution.py:119
  207.4 28.7 %all-gather.7.cloned.1.call-done = bf16[96,128,384]{2,1,0:T(8,128)(2,1)} async-done(((bf16[6,128,384]{2,1,0:T(8,128)(2,1)}), bf16[96,128,384]{2,1,0:T(8,128)(2,1)}) %all-gather.7.cloned.1.call-update) | async-done | bytes 9437200 | tf_op jit(solution)/shard_map/all_gather | solution.py:108
  236.1 7.8 %gather_fusion = bf16[60,128,384]{2,1,0:T(8,128)(2,1)} fusion(bf16[96,128,384]{2,1,0:T(8,128)(2,1)} %all-gather.7.cloned.1.call-done, s32[1024]{0:T(1024)S(1)} %pad_clamp_fusion.1), kind=kCustom, calls=%fused_computation | custom fusion | bytes 11796720 | tf_op jit(solution)/shard_map/gather | solution.py:111
  243.9 15.8 %reshape.243 = bf16[6,1280,3,128]{3,2,1,0:T(4,128)(2,1)} reshape(bf16[60,128,384]{2,1,0:T(8,128)(2,1)} %gather_fusion) | data formatting | bytes 11796480 | tf_op jit(solution)/shard_map/reshape | solution.py:111
  259.7 9.2 %fusion.19 = bf16[6,128,3,128]{1,3,2,0:T(8,128)(2,1)S(1)} fusion(f32[6,3,128,1280]{3,2,1,0:T(8,128)} %get-tuple-element.24, f32[6,3,128]{2,1,0:T(4,128)S(1)} %get-tuple-element.23, bf16[6,1280,3,128]{3,2,1,0:T(4,128)(2,1)} %reshape.243), kind=kOutput, calls=%fused_computation.21 | convolution fusion | flops 761167872 | bytes 18293760 | tf_op jit(solution)/shard_map/nhqk,nkhd->nqhd/dot_general | solution.py:121
  268.9 0.4 copy.49
  269.3 8.8 %convolution_convert_fusion = bf16[768,5120]{1,0:T(8,128)(2,1)} fusion(bf16[384,5120]{1,0:T(8,128)(2,1)} %param.15, bf16[48,8,6,128]{3,2,1,0:T(8,128)(2,1)S(1)} %bitcast.68), kind=kOutput, calls=%fused_computation.11 | convolution fusion | flops 3023831040 | bytes 12386304 | tf_op jit(solution)/shard_map/dot_general | solution.py:131
  278.2 10.7 %copy.54 = bf16[768,5120]{0,1:T(8,128)(2,1)} copy(bf16[768,5120]{1,0:T(8,128)(2,1)} %convolution_convert_fusion) | data formatting | bytes 15728640
  288.8 0.0 reduce-scatter.4.cloned.1.call-update
  288.8 0.8 copy-done.6
  289.6 0.2 convolution_convert_fusion.2
  289.8 14.6 %all-gather = bf16[6144,64]{0,1:T(8,128)(2,1)S(1)} all-gather(bf16[768,64]{0,1:T(8,128)(2,1)S(1)} %convolution_convert_fusion.2), channel_id=2, replica_groups=mesh['frame'=16,'head'=8] {'head'}, dimensions={0}, use_global_device_ids=true | all-gather | bytes 884736 | tf_op jit(solution)/shard_map/all_gather | solution.py:13
  304.4 0.1 copy.57
  304.6 0.6 bitcast_reduce_fusion
  305.2 34.7 %reduce-scatter.4.cloned.1.call-done = bf16[640,768]{1,0:T(8,128)(2,1)} async-done(((bf16[5120,768]{1,0:T(8,128)(2,1)}), bf16[640,768]{1,0:T(8,128)(2,1)}) %reduce-scatter.4.cloned.1.call-update) | async-done | bytes 983056
  339.9 1.5 copy.55
  341.4 1.4 add_convert_fusion
  (17 shorter events, 0.1 us)
Async XLA Ops:
  6.5 52.6 %copy-start = (bf16[5120,192]{0,1:T(8,128)(2,1)S(1)}, bf16[5120,192]{0,1:T(8,128)(2,1)}, u32[]{:S(2)}) copy-start(bf16[5120,192]{0,1:T(8,128)(2,1)} %param.13) | copy-start | bytes 5898244
  6.5 52.6 %all-gather.5.cloned.1.call-start = ((), (), s32[]{:S(2)}) async-start(), calls=%async_computation.1 | async-start | bytes 8847360 | tf_op jit(solution)/shard_map/all_gather | solution.py:78
  7.3 151.5 %all-gather.9.cloned.1.call-start = ((), (), s32[]{:S(2)}) async-start(), calls=%async_computation.3 | async-start | bytes 10027008 | tf_op jit(solution)/shard_map/all_gather | solution.py:107
  27.4 37.9 %copy-start.4 = (bf16[64,3,384]{2,0,1:T(8,128)(2,1)S(1)}, bf16[64,3,384]{2,0,1:T(8,128)(2,1)}, u32[]{:S(2)}) copy-start(bf16[64,3,384]{2,0,1:T(8,128)(2,1)} %param.14) | copy-start | bytes 442372
  59.2 6.8 %copy-start.2 = (bf16[5120,3,384]{0,2,1:T(8,128)(2,1)S(1)}, bf16[5120,3,384]{0,2,1:T(8,128)(2,1)}, u32[]{:S(2)}) copy-start(bf16[5120,3,384]{0,2,1:T(8,128)(2,1)} %copy.37) | copy-start | bytes 35389444
  79.3 1.8 copy-start.3
  79.5 6.4 %copy-start.7 = (s32[96,10]{0,1:T(8,128)S(1)}, s32[96,10]{0,1:T(8,128)}, u32[]{:S(2)}) copy-start(s32[96,10]{0,1:T(8,128)} %param.11) | copy-start | bytes 11524
  83.2 152.9 %all-gather.7.cloned.1.call-start = ((), (), s32[]{:S(2)}) async-start(), calls=%async_computation.2 | async-start | bytes 10027008 | tf_op jit(solution)/shard_map/all_gather | solution.py:108
  85.6 254.2 %reduce-scatter.4.cloned.1.call-start = ((), (), s32[]{:S(2)}) async-start(), calls=%async_computation.4 | async-start | bytes 8847360
  288.8 0.8 copy-start.6
  288.8 52.6 %copy-start.5 = (bf16[64,640]{1,0:T(8,128)(2,1)S(1)}, bf16[64,640]{1,0:T(8,128)(2,1)}, u32[]{:S(2)}) copy-start(bf16[64,640]{1,0:T(8,128)(2,1)} %param.17) | copy-start | bytes 245764
  289.6 53.2 %copy-start.1 = (bf16[5120,192]{0,1:T(8,128)(2,1)S(1)}, bf16[5120,192]{0,1:T(8,128)(2,1)}, u32[]{:S(2)}) copy-start(bf16[5120,192]{0,1:T(8,128)(2,1)} %param.13) | copy-start | bytes 5898244
Sparse Core Ops, SparseCore 0:
  9.0 50.0 all-gather.4
  83.3 75.4 all-gather.8
  160.9 75.1 all-gather.6
  289.0 50.8 reduce-scatter.3
